TPU v7x, 256 devices: a whole 4x4x8 slice. The times are simulated.
256 devices in a mesh: seq: 32 (over y, z), head: 8 (over x, core).
Axes of the slice: x: 4, y: 4, z: 8, core: 2. Of those that a mesh axis runs over, the one named last changes fastest.
Arguments:
- queries: bfloat16 [8192, 32, 128], P('seq', 'head'), may hold values from -42 to 42, as said below
- keys: bfloat16 [8192, 8, 128], P('seq', 'head'), may hold values from -6 to 6
- values: bfloat16 [8192, 8, 128], P('seq', 'head'), may hold values from -6 to 6
- feat_q: bfloat16 [32, 128, 128], P('head'), may hold values from -0.5 to 0.5
- feat_k: bfloat16 [32, 128, 128], P('head'), may hold values from -0.5 to 0.5
- samples: int32 [32], replicated, may hold values from 0 to 1
Outputs:
- student: bfloat16 [8192, 32, 128], P('seq', 'head')
- teacher: float32 [32, 128, 32, 128], P('seq', None, 'head')
- loss: float32 [], replicated
Inputs may be any that keep to these rules, and one draw needn't show every extreme that they name: `queries`: query vectors; some may be large multiples of earlier key vectors.
All inputs are finite; a program needn't handle non-finite values.
Results may differ from a plain program's by a relative error of at most 0.009.
Values may be sent and summed in bfloat16 or wider, within the bound.
No kernel may reach another device: no remote copies, remote signals or barrier semaphores. Data moves between devices by JAX's collectives and lax.ppermute only.
A program may use at most 64 MiB of HBM per device.

v0:
```python
import jax
import jax.numpy as jnp
from jax import lax
from jax.sharding import PartitionSpec as P

HD = 128
FEAT = 128
QH_DEV = 4
BLOCK = 128


PRECISE = lax.Precision.HIGHEST
MASKED = -1e30


def prefix(x, axis, combine, identity):
    count, mine = (lax.axis_size(axis), lax.axis_index(axis))
    everything = jax.tree.map(
        lambda part, kind: lax.all_gather(part.astype(kind), axis), x, (jnp.bfloat16, jnp.bfloat16)
    )
    start = jax.tree.map(
        lambda part, zero: jnp.broadcast_to(jnp.asarray(zero, part.dtype), part.shape), x, identity
    )

    def lap(k, before):
        reached = k < mine
        new = combine(
            before, jax.tree.map(lambda part, own: part[k].astype(own.dtype), everything, x)
        )
        return jax.tree.map(lambda a, b: jnp.where(reached, a, b), new, before)

    return lax.fori_loop(0, count, lap, start)


def features(logits):
    return jnp.concatenate(
        [jax.nn.softmax(logits, axis=-1), jax.nn.softmax(-logits, axis=-1)], axis=-1
    ).astype(jnp.bfloat16)


def add_pair(earlier, later):
    return (earlier[0] + later[0], earlier[1] + later[1])


def absorb(running, query_rows, row_places, key_part, value_part, inv_root):
    best, totals, accum = running
    scores = (
        jnp.einsum("bhd,kd->hbk", query_rows, key_part, preferred_element_type=jnp.float32)
        * inv_root
    )
    key_places = jnp.arange(key_part.shape[0])
    live = (key_places[None, :] <= row_places[:, None])[None]
    peak = jnp.max(jnp.where(live, scores, MASKED), axis=-1)
    newtop = jnp.maximum(best, peak)
    weights = jnp.where(live, jnp.exp(scores - newtop[..., None]), 0.0)
    totals = jnp.sum(weights, axis=-1)
    accum = jnp.einsum(
        "hbk,kd->hbd", weights.astype(jnp.bfloat16), value_part, preferred_element_type=jnp.float32
    )
    return (newtop, totals, accum)


def on_device(queries, keys, values, feat_q, feat_k, samples):
    tok_rows, head_count, head_width = queries.shape
    stretch_count = lax.axis_size("seq")
    inv_root = 1.0 / head_width**0.5
    key_rows = keys[:, 0]
    value_rows = values[:, 0]
    phi_q = features(
        jnp.einsum("lhd,hdf->lhf", queries, feat_q, preferred_element_type=jnp.float32)
    )
    phi_k = features(
        jnp.einsum("ld,hdf->lhf", key_rows, feat_k, preferred_element_type=jnp.float32)
    )
    span_rows = min(tok_rows, 512)
    block_count = tok_rows // span_rows
    fq_blocks = phi_q.reshape(block_count, span_rows, head_count, 2 * FEAT)
    fk_blocks = phi_k.reshape(block_count, span_rows, head_count, 2 * FEAT)
    value_blocks = value_rows.reshape(block_count, span_rows, head_width)
    block_states = jnp.einsum(
        "nlhf,nld->nhfd", fk_blocks, value_blocks, preferred_element_type=jnp.float32
    )
    block_totals = jnp.sum(fk_blocks, axis=1, dtype=jnp.float32)
    local_state = jnp.sum(block_states, axis=0)
    local_total = jnp.sum(block_totals, axis=0)
    empty_state = jnp.zeros_like(local_state)
    empty_total = jnp.zeros_like(local_total)
    enter_state, enter_total = prefix(
        (local_state, local_total), "seq", add_pair, (empty_state, empty_total)
    )
    before_states = jnp.cumsum(block_states, axis=0) - block_states
    before_totals = jnp.cumsum(block_totals, axis=0) - block_totals
    states_in = enter_state[None] + before_states
    totals_in = enter_total[None] + before_totals
    causal = jnp.arange(span_rows)[:, None] >= jnp.arange(span_rows)[None, :]
    kernel = jnp.einsum("nihf,njhf->nhij", fq_blocks, fk_blocks, preferred_element_type=jnp.float32)
    kernel = jnp.where(causal[None, None], kernel, 0.0)
    kernel_low = kernel.astype(jnp.bfloat16)
    numer = jnp.einsum(
        "nhij,njd->nihd", kernel_low, value_blocks, preferred_element_type=jnp.float32
    )
    numer = numer + jnp.einsum(
        "nihf,nhfd->nihd",
        fq_blocks,
        states_in,
        precision=PRECISE,
        preferred_element_type=jnp.float32,
    )
    denom = jnp.transpose(jnp.sum(kernel, axis=3), (0, 2, 1)) + jnp.einsum(
        "nihf,nhf->nih", fq_blocks, totals_in, precision=PRECISE, preferred_element_type=jnp.float32
    )
    student = (
        (numer / denom[..., None]).astype(jnp.bfloat16).reshape(tok_rows, head_count, head_width)
    )
    device_index = lax.axis_index("seq")
    picked = samples[device_index]
    row_first = device_index * tok_rows + picked * BLOCK
    query_rows = lax.dynamic_slice_in_dim(queries, picked * BLOCK, BLOCK, 0)
    row_places = row_first + jnp.arange(BLOCK)
    fresh = (
        jnp.full((head_count, BLOCK), MASKED, jnp.float32),
        jnp.zeros((head_count, BLOCK), jnp.float32),
        jnp.zeros((head_count, BLOCK, head_width), jnp.float32),
    )
    key_part = lax.all_gather(keys, "seq", axis=0, tiled=True)
    value_part = lax.all_gather(values, "seq", axis=0, tiled=True)
    best, totals, accum = lax.cond(
        jnp.int32(0) <= row_first + BLOCK - 1,
        lambda kept: absorb(
            kept, query_rows, row_places, key_part[:, 0], value_part[:, 0], inv_root
        ),
        lambda kept: kept,
        fresh,
    )
    mixed = accum / totals[..., None]
    teacher = jnp.transpose(mixed, (1, 0, 2))[None]
    student_rows = lax.dynamic_slice_in_dim(student, picked * BLOCK, BLOCK, 0).astype(jnp.float32)
    gap = student_rows - teacher[0]
    entry_count = stretch_count * lax.axis_size("head") * BLOCK * QH_DEV * HD
    loss = lax.psum(jnp.sum(gap * gap), ("seq", "head")) / entry_count
    return (student, teacher, loss)


def solution(mesh):
    in_specs = (
        P("seq", "head", None),
        P("seq", "head", None),
        P("seq", "head", None),
        P("head", None, None),
        P("head", None, None),
        P(),
    )
    out_specs = (P("seq", "head", None), P("seq", None, "head", None), P())
    return jax.shard_map(
        on_device, mesh=mesh, in_specs=in_specs, out_specs=out_specs, check_vma=False
    )
```

profile of v0, /device:TPU:1, one launch (start us, length us, event | category | flops | bytes accessed | tf_op | source)
XLA Modules:
  0.0 396.0 jit_solution(10727178128986259759)
XLA Ops:
  9.7 1.2 fusion.61
  10.9 1.1 fusion.43
  12.6 1.8 fusion.65
  14.5 1.3 dynamic_slice.26
  16.7 42.3 %all-gather.2 = bf16[32,4,256]{2,1,0:T(4,128)(2,1)S(1)} all-gather(bf16[1,4,256]{2,1,0:T(4,128)(2,1)S(1)} %convert_bitcast_fusion), channel_id=3, replica_groups=mesh['seq'=32,'head'=8] {'seq'}, dimensions={0}, use_global_device_ids=true | all-gather | bytes 67584 | tf_op jit(solution)/shard_map/all_gather | solution.py:19
  59.1 1.3 fusion.66
  60.4 1.3 fusion.69
  62.2 25.6 %all-gather.7.cloned.1.call-done = bf16[8192,1,128]{2,0,1:T(8,128)(2,1)} async-done(((bf16[256,1,128]{2,0,1:T(8,128)(2,1)}), bf16[8192,1,128]{2,0,1:T(8,128)(2,1)}) %all-gather.7.cloned.1.call-update) | async-done | bytes 2097168 | tf_op jit(solution)/shard_map/all_gather | solution.py:125
  87.8 77.7 %all-gather.9.cloned.1.call-done = bf16[8192,1,128]{2,0,1:T(8,128)(2,1)} async-done(((bf16[256,1,128]{2,0,1:T(8,128)(2,1)}), bf16[8192,1,128]{2,0,1:T(8,128)(2,1)}) %all-gather.9.cloned.1.call-update) | async-done | bytes 2097168 | tf_op jit(solution)/shard_map/all_gather | solution.py:126
  165.5 16.0 %conditional.1 = (f32[4,128]{1,0:T(4,128)S(1)}, f32[4,128,128]{2,1,0:T(8,128)S(1)}) conditional(s32[]{:T(128)} %convert_element_type.94, () %tuple.33, (s32[]{:T(128)}, s32[128]{0:T(128)S(1)}, bf16[256,4,128]{2,1,0:T(4,128)(2,1)}, s32[]{:T(128)}, bf16[8192,1,128]{2,0,1:T(8,128)(2,1)}, /*index=5*/bf16[8192,1,128]{2,0,1:T(8,128)(2,1)}) %tuple.34), branch_computations={%region_12.13_spmd, %region_13.0_spmd} | conditional | flops 2194669056 | bytes 59651608 | solution.py:127
  167.2 4.8 %fusion = (f32[4,128]{1,0:T(4,128)S(1)}, f32[128,4,8192]{2,0,1:T(8,128)S(1)}) fusion(pred[128,8192]{1,0:T(8,128)(4,1)S(1)} %iota_compare_fusion, bf16[8192,1,128]{2,0,1:T(8,128)(2,1)} %get-tuple-element.140, bf16[256,4,128]{2,0,1:T(8,128)(2,1)S(1)} %copy.30, s32[]{:T(128)} %get-tuple-element.139), kind=kOutput, calls=%fused_computation.2 | convolution fusion | flops 1086324224 | bytes 20056068 | tf_op jit(solution)/shard_map/cond/branch_1_fun/bhd,kd->hbk/dot_general | solution.py:48
  172.0 4.8 %fusion.5 = f32[4,128,128]{2,1,0:T(8,128)S(1)} fusion(f32[128,4,8192]{2,0,1:T(8,128)S(1)} %get-tuple-element.205, f32[4,128]{1,0:T(4,128)S(1)} %broadcast_maximum_fusion, pred[128,8192]{1,0:T(8,128)(4,1)S(1)} %iota_compare_fusion, bf16[8192,1,128]{2,0,1:T(8,128)(2,1)} %get-tuple-element.141), kind=kOutput, calls=%fused_computation.7 | convolution fusion | flops 1090519040 | bytes 20187136 | tf_op jit(solution)/shard_map/cond/branch_1_fun/hbk,kd->hbd/dot_general | solution.py:57
  176.8 4.6 %fusion.4 = f32[4,128]{1,0:T(4,128)S(1)} fusion(f32[128,4,8192]{2,0,1:T(8,128)S(1)} %get-tuple-element.205, f32[4,128]{1,0:T(4,128)S(1)} %broadcast_maximum_fusion, pred[128,8192]{1,0:T(8,128)(4,1)S(1)} %iota_compare_fusion), kind=kLoop, calls=%fused_computation.6 | loop fusion | flops 16776704 | bytes 17829888 | tf_op jit(solution)/shard_map/cond/branch_1_fun/reduce_sum | solution.py:56
  181.6 86.1 %all-gather.11.cloned.1.call-done = bf16[128,256,128]{2,1,0:T(8,128)(2,1)} async-done(((bf16[4,256,128]{2,1,0:T(8,128)(2,1)}), bf16[128,256,128]{2,1,0:T(8,128)(2,1)}) %all-gather.11.cloned.1.call-update) | async-done | bytes 8388624 | tf_op jit(solution)/shard_map/all_gather | solution.py:19
  267.6 40.8 %while.16 = (s32[]{:T(128)}, f32[4,256,128]{2,1,0:T(8,128)S(1)}, f32[4,256]{1,0:T(4,128)S(1)}, s32[]{:T(128)}, bf16[32,4,256,128]{3,2,1,0:T(8,128)(2,1)}, /*inde...) while((s32[]{:T(128)}, f32[4,256,128]{2,1,0:T(8,128)S(1)}, f32[4,256]{1,0:T(4,128)S(1)}, ...), condition=%wide.region_10.0_spmd.clone, body=%wide.region_9.0_spmd.clone.sunk | while | flops 528388 | bytes 1321083 | solution.py:32
  267.6 1.2 add_select_fusion.4
  268.9 1.2 add_select_fusion.4
  270.2 1.2 add_select_fusion.4
  271.5 1.2 add_select_fusion.4
  272.7 1.2 add_select_fusion.4
  274.0 1.2 add_select_fusion.4
  275.3 1.2 add_select_fusion.4
  276.6 1.2 add_select_fusion.4
  277.8 1.2 add_select_fusion.4
  279.1 1.2 add_select_fusion.4
  280.4 1.2 add_select_fusion.4
  281.7 1.2 add_select_fusion.4
  282.9 1.2 add_select_fusion.4
  284.2 1.2 add_select_fusion.4
  285.5 1.2 add_select_fusion.4
  286.8 1.2 add_select_fusion.4
  288.0 1.2 add_select_fusion.4
  289.3 1.2 add_select_fusion.4
  290.6 1.2 add_select_fusion.4
  291.9 1.2 add_select_fusion.4
  293.2 1.2 add_select_fusion.4
  294.4 1.2 add_select_fusion.4
  295.7 1.2 add_select_fusion.4
  297.0 1.2 add_select_fusion.4
  298.3 1.2 add_select_fusion.4
  299.5 1.2 add_select_fusion.4
  300.8 1.2 add_select_fusion.4
  302.1 1.2 add_select_fusion.4
  303.4 1.2 add_select_fusion.4
  304.6 1.2 add_select_fusion.4
  305.9 1.2 add_select_fusion.4
  307.2 1.2 add_select_fusion.4
  311.5 75.3 %psum.7 = f32[]{:T(128)} all-reduce(f32[]{:T(128)} %fusion.37), channel_id=1, replica_groups=mesh['seq'=32,'head'=8] {'seq','head'}, use_global_device_ids=true, to_apply=%region_17.18 | all-reduce | flops 1 | bytes 8 | tf_op jit(solution)/shard_map/psum | solution.py:140
  (66 shorter events, 10.2 us)
Async XLA Ops:
  7.2 51.9 %copy-start = (bf16[4,128,128]{2,1,0:T(8,128)(2,1)S(1)}, bf16[4,128,128]{2,1,0:T(8,128)(2,1)}, u32[]{:S(2)}) copy-start(bf16[4,128,128]{2,1,0:T(8,128)(2,1)} %param.13) | copy-start | bytes 393220
  7.2 80.6 %all-gather.7.cloned.1.call-start = ((), (), s32[]{:S(2)}) async-start(), calls=%async_computation | async-start | bytes 2162688 | tf_op jit(solution)/shard_map/all_gather | solution.py:125
  7.9 157.5 %all-gather.9.cloned.1.call-start = ((), (), s32[]{:S(2)}) async-start(), calls=%async_computation.1 | async-start | bytes 2162688 | tf_op jit(solution)/shard_map/all_gather | solution.py:126
  8.7 259.0 %all-gather.11.cloned.1.call-start = ((), (), s32[]{:S(2)}) async-start(), calls=%async_computation.2 | async-start | bytes 8650752 | tf_op jit(solution)/shard_map/all_gather | solution.py:19
  165.5 144.0 %copy-start.1 = (bf16[256,1,128]{2,0,1:T(8,128)(2,1)S(1)}, bf16[256,1,128]{2,0,1:T(8,128)(2,1)}, u32[]{:S(2)}) copy-start(bf16[256,1,128]{2,0,1:T(8,128)(2,1)} %param.12) | copy-start | bytes 196612
Sparse Core Ops, SparseCore 0:
  10.6 77.1 all-gather.6
  90.4 75.0 all-gather.8
  168.6 98.9 all-gather.10
where the time goes:
time: 397 us; the launch traced here: 396 us
  waiting for transfers between devices  191 us (48%)
  blocking collectives  118 us (30%)
  other arithmetic  47.1 us (12%)
  matrix products  18.1 us (5%)
  between operations  16.4 us (4%)
  local copies, waits for them, and re-layouts  5.16 us (1%)
    all_gather x1, waiting for transfers between devices, prefix(): lax.all_gather(part.astype(kind), axis)  86.1 us
    all_gather x1, waiting for transfers between devices, on_device(): value_part = lax.all_gather(values, 'seq', axis=0, tiled=True)  77.7 us
    psum x1, blocking collectives, on_device(): loss = lax.psum(jnp.sum(gap * gap), ('seq', 'head')) / entry_count  75.3 us
    all_gather x1, blocking collectives, prefix(): lax.all_gather(part.astype(kind), axis)  42.3 us
    select_n x64, other arithmetic, lap(): return jax.tree.map(lambda a, b: jnp.where(reached, a, b), new, before)  40 us
    all_gather x1, waiting for transfers between devices, on_device(): key_part = lax.all_gather(keys, 'seq', axis=0, tiled=True)  25.6 us
  transfers between devices with their start and end apart: 3, of which 3 were waited for; matrix products, arithmetic and copies ran while one was open for 7% of the time, Pallas kernels for 0%

commit v1 on v0

v1 whole, which is shorter than its diff:
```python
import jax
import jax.numpy as jnp
from jax import lax
from jax.experimental import pallas as pl
from jax.experimental.pallas import tpu as pltpu
from jax.sharding import PartitionSpec as P

HD = 128
FEAT = 128
QH_DEV = 4
BLOCK = 128
MASKED = -1e30
F32 = jnp.float32


def features(logits):
    return jnp.concatenate(
        [jax.nn.softmax(logits, axis=-1), jax.nn.softmax(-logits, axis=-1)], axis=-1
    ).astype(jnp.bfloat16)


def prefix_states(state, total):
    count = lax.axis_size("seq")
    heads, feats, width = state.shape
    rows = heads * feats // count
    parts = jnp.concatenate(
        [
            state.reshape(count, rows, width),
            jnp.pad(total.reshape(count, 1, rows), ((0, 0), (0, 15), (0, width - rows))),
        ],
        axis=1,
    ).astype(jnp.bfloat16)
    mine = lax.all_to_all(parts, "seq", 0, 0)
    earlier = (jnp.arange(count)[:, None] > jnp.arange(count)[None, :]).astype(jnp.bfloat16)
    sums = jnp.einsum("st,trw->srw", earlier, mine, preferred_element_type=F32).astype(jnp.bfloat16)
    back = lax.all_to_all(sums, "seq", 0, 0)
    return (
        back[:, :rows].reshape(heads, feats, width),
        back[:, rows, :rows].reshape(heads, feats),
    )


KEYS_STEP = 1024


def teach_step(place_ref, query_ref, pair_ref, out_ref, best_ref, total_ref, accum_ref):
    step = pl.program_id(0)
    row_first = place_ref[0]
    key_first = step * KEYS_STEP
    rows = query_ref.shape[0]
    width = query_ref.shape[1]

    @pl.when(step == 0)
    def _():
        best_ref[...] = jnp.full(best_ref.shape, MASKED, F32)
        total_ref[...] = jnp.zeros(total_ref.shape, F32)
        accum_ref[...] = jnp.zeros(accum_ref.shape, F32)

    def absorb(masked):
        key_part = pair_ref[:, :width]
        value_part = pair_ref[:, width:]
        scores = lax.dot_general(
            query_ref[...], key_part, (((1,), (1,)), ((), ())), preferred_element_type=F32
        ) * (1.0 / width**0.5)
        if masked:
            place = row_first + lax.rem(lax.broadcasted_iota(jnp.int32, scores.shape, 0), BLOCK)
            live = key_first + lax.broadcasted_iota(jnp.int32, scores.shape, 1) <= place
            scores = jnp.where(live, scores, MASKED)
        best = best_ref[...]
        newtop = jnp.maximum(best, jnp.max(scores, axis=1, keepdims=True))
        fade = jnp.exp(best - newtop)
        weights = jnp.exp(scores - newtop)
        total_ref[...] = fade * total_ref[...] + jnp.sum(weights, axis=1, keepdims=True)
        accum_ref[...] = fade * accum_ref[...] + jnp.dot(
            weights.astype(jnp.bfloat16), value_part, preferred_element_type=F32
        )
        best_ref[...] = newtop

    @pl.when(key_first + KEYS_STEP <= row_first)
    def _():
        absorb(False)

    @pl.when((key_first + KEYS_STEP > row_first) & (key_first <= row_first + BLOCK - 1))
    def _():
        absorb(True)

    @pl.when(step == pl.num_programs(0) - 1)
    def _():
        out_ref[...] = accum_ref[...] / total_ref[...]


def teach(row_first, query_rows, gathered):
    rows, width = query_rows.shape
    return pl.pallas_call(
        teach_step,
        out_shape=jax.ShapeDtypeStruct((rows, width), F32),
        grid_spec=pltpu.PrefetchScalarGridSpec(
            num_scalar_prefetch=1,
            grid=(gathered.shape[0] // KEYS_STEP,),
            in_specs=[
                pl.BlockSpec((rows, width), lambda i, place: (0, 0)),
                pl.BlockSpec((KEYS_STEP, 2 * width), lambda i, place: (i, 0)),
            ],
            out_specs=pl.BlockSpec((rows, width), lambda i, place: (0, 0)),
            scratch_shapes=[
                pltpu.VMEM((rows, 1), F32),
                pltpu.VMEM((rows, 1), F32),
                pltpu.VMEM((rows, width), F32),
            ],
        ),
    )(row_first.reshape(1), query_rows, gathered)


def on_device(queries, keys, values, feat_q, feat_k, samples):
    tok_rows, head_count, head_width = queries.shape
    stretch_count = lax.axis_size("seq")
    both = jnp.concatenate([keys[:, 0], values[:, 0]], axis=1)
    gathered = lax.all_gather(both, "seq", axis=0, tiled=True)
    key_rows = keys[:, 0]
    value_rows = values[:, 0]
    phi_q = features(jnp.einsum("lhd,hdf->hlf", queries, feat_q, preferred_element_type=F32))
    phi_k = features(jnp.einsum("ld,hdf->hlf", key_rows, feat_k, preferred_element_type=F32))
    state = jnp.einsum("hlf,ld->hfd", phi_k, value_rows, preferred_element_type=F32)
    total = jnp.sum(phi_k, axis=1, dtype=F32)
    enter_state, enter_total = prefix_states(state, total)
    causal = jnp.arange(tok_rows)[:, None] >= jnp.arange(tok_rows)[None, :]
    kernel = jnp.einsum("hif,hjf->hij", phi_q, phi_k, preferred_element_type=F32)
    kernel = jnp.where(causal[None], kernel, 0.0)
    numer = jnp.einsum("hij,jd->hid", kernel.astype(jnp.bfloat16), value_rows, preferred_element_type=F32)
    numer = numer + jnp.einsum("hif,hfd->hid", phi_q, enter_state, preferred_element_type=F32)
    denom = jnp.sum(kernel, axis=2) + jnp.sum(phi_q.astype(F32) * enter_total.astype(F32)[:, None, :], axis=2)
    student = jnp.transpose((numer / denom[..., None]).astype(jnp.bfloat16), (1, 0, 2))
    device_index = lax.axis_index("seq")
    picked = samples[device_index]
    row_first = device_index * tok_rows + picked * BLOCK
    query_rows = lax.dynamic_slice_in_dim(queries, picked * BLOCK, BLOCK, 0)
    query_stack = jnp.transpose(query_rows, (1, 0, 2)).reshape(head_count * BLOCK, head_width)
    mixed = teach(row_first, query_stack, gathered).reshape(head_count, BLOCK, head_width)
    teacher = jnp.transpose(mixed, (1, 0, 2))
    student_rows = lax.dynamic_slice_in_dim(student, picked * BLOCK, BLOCK, 0).astype(F32)
    gap = student_rows - teacher
    group = stretch_count * lax.axis_size("head")
    entry_count = group * BLOCK * QH_DEV * HD
    mine = jnp.sum(gap * gap)
    shared = lax.all_to_all(jnp.broadcast_to(mine, (group, 1, 128)), ("seq", "head"), 0, 0)
    loss = jnp.sum(shared[:, 0, 0]) / entry_count
    return (student, teacher[None], loss)


def solution(mesh):
    in_specs = (
        P("seq", "head", None),
        P("seq", "head", None),
        P("seq", "head", None),
        P("head", None, None),
        P("head", None, None),
        P(),
    )
    out_specs = (P("seq", "head", None), P("seq", None, "head", None), P())
    return jax.shard_map(
        on_device, mesh=mesh, in_specs=in_specs, out_specs=out_specs, check_vma=False
    )
```

time: 397 us -> 149 us (0.38)
  waiting for transfers between devices: 191 us -> 65.4 us
  blocking collectives: 118 us -> 0 us
  other arithmetic: 47.1 us -> 4.96 us
  starting transfers between devices: 0.11 us -> 41.8 us
  matrix products: 18.1 us -> 4.92 us
  Pallas kernels: 0 us -> 7.2 us
    all_gather x3 -> x1, waiting for transfers between devices: 189 us -> 34.2 us  [on_device(): gathered = lax.all_gather(both, 'seq', axis=0, tiled=True)]
    psum x1 -> x0, blocking collectives: 75.3 us -> none  [on_device(): loss = lax.psum(jnp.sum(gap * gap), ('seq', 'head')) / entry_count]
    all_gather x1 -> x0, blocking collectives: 42.3 us -> none  [prefix(): lax.all_gather(part.astype(kind), axis)]
    all_to_all x0 -> x3, starting transfers between devices: none -> 41.8 us  [the longest x1 21.5 us: on_device(): lax.all_to_all(jnp.broadcast_to(mine, (group, 1, 128)), ('seq', 'head'),...]
    select_n x64 -> x0, other arithmetic: 40 us -> none  [lap(): return jax.tree.map(lambda a, b: jnp.where(reached, a, b), new, before)]
    all_to_all x0 -> x3, waiting for transfers between devices: none -> 31.1 us  [the longest x1 10.7 us: prefix_states(): mine = lax.all_to_all(parts, 'seq', 0, 0)]
    dot_general x7 -> x5, matrix products: 13.2 us -> 1.79 us  [the longest x1 0.46 us: on_device(): jnp.einsum('hlf,ld->hfd', phi_k, value_rows, preferred_element_type=F32)]
    pallas_call x0 -> x1, Pallas kernels: none -> 7.2 us  [teach(): pl.pallas_call(teach_step, out_shape=jax.ShapeDtypeStruct((rows, width),...]
  transfers between devices with their start and end apart: 3 -> 4, of which waited for: 3 -> 4; matrix products, arithmetic and copies ran while one was open for 7% -> 8% of each run, Pallas kernels for 0% -> 0%
where the time goes in v1:
time: 149 us; the launch traced here: 148 us
  waiting for transfers between devices  65.4 us (44%)
  starting transfers between devices  41.8 us (28%)
  between operations  16.7 us (11%)
  local copies, waits for them, and re-layouts  7.43 us (5%)
  Pallas kernels  7.2 us (5%)
  other arithmetic  4.96 us (3%)
  matrix products  4.92 us (3%)
    all_gather x1, waiting for transfers between devices, on_device(): gathered = lax.all_gather(both, 'seq', axis=0, tiled=True)  34.2 us
    all_to_all x1, starting transfers between devices, on_device(): lax.all_to_all(jnp.broadcast_to(mine, (group, 1, 128)), ('seq', 'head'),...  21.5 us
    all_to_all x1, starting transfers between devices, prefix_states(): mine = lax.all_to_all(parts, 'seq', 0, 0)  12 us
    all_to_all x1, waiting for transfers between devices, prefix_states(): mine = lax.all_to_all(parts, 'seq', 0, 0)  10.7 us
    all_to_all x1, waiting for transfers between devices, prefix_states(): back = lax.all_to_all(sums, 'seq', 0, 0)  10.3 us
    all_to_all x1, waiting for transfers between devices, on_device(): lax.all_to_all(jnp.broadcast_to(mine, (group, 1, 128)), ('seq', 'head'),...  10.1 us
    all_to_all x1, starting transfers between devices, prefix_states(): back = lax.all_to_all(sums, 'seq', 0, 0)  8.3 us
    pallas_call x1, Pallas kernels, teach(): pl.pallas_call(teach_step, out_shape=jax.ShapeDtypeStruct((rows, width),...  7.2 us
  transfers between devices with their start and end apart: 4, of which 4 were waited for; matrix products, arithmetic and copies ran while one was open for 8% of the time, Pallas kernels for 0%

profile of v1, /device:TPU:1, one launch (start us, length us, event | category | flops | bytes accessed | tf_op | source)
XLA Modules:
  0.0 148.4 jit_solution(17945552878526933659)
XLA Ops:
  7.2 0.0 copy-start
  7.2 0.0 copy-start.1
  7.2 0.0 copy-start.4
  7.2 0.0 copy-start.2
  7.2 0.0 copy-start.3
  7.2 0.0 all-gather.2.cloned.1.call-start
  7.3 1.6 %pad_maximum_fusion.4 = bf16[256,256]{1,0:T(8,128)(2,1)} fusion(bf16[256,128]{1,0:T(8,128)(2,1)} %bitcast.74, bf16[256,128]{1,0:T(8,128)(2,1)} %bitcast.73), kind=kLoop, calls=%fused_computation.46 | loop fusion | flops 262144 | bytes 262144 | tf_op jit(solution)/shard_map/concatenate | solution.py:117
  8.9 0.0 all-gather.2.cloned.1.call-update
  8.9 0.0 copy-done
  8.9 1.2 fusion.45
  10.1 1.2 fusion.48
  11.3 0.1 divide_convert_fusion
  11.4 0.2 pad_maximum_fusion.1
  11.7 0.1 reshape.58
  11.7 0.0 copy-done.1
  11.7 0.5 convolution_convert_fusion.1
  12.3 0.9 copy.65
  13.2 12.0 %all-to-all-start = ((bf16[32,48,128]{2,1,0:T(8,128)(2,1)}), bf16[32,48,128]{2,1,0:T(8,128)(2,1)S(1)}, u32[]{:S(2)}, u32[]{:S(2)}) async-start(bf16[32,48,128]{2,1,0:T(8,128)(2,1)} %copy.65), calls=%async_computation | async-start | bytes 786432 | tf_op jit(solution)/shard_map/all_to_all | solution.py:33
  25.2 0.0 copy-done.4
  25.2 0.6 dynamic_slice.9
  26.5 0.0 copy-done.2
  26.5 0.1 dynamic-slice_bitcast_fusion
  26.5 0.0 copy-done.3
  26.5 0.4 fusion.51
  26.9 10.7 %all-to-all-done = bf16[32,48,128]{2,1,0:T(8,128)(2,1)S(1)} async-done(((bf16[32,48,128]{2,1,0:T(8,128)(2,1)}), bf16[32,48,128]{2,1,0:T(8,128)(2,1)S(1)}, u32[]{:S(2)}, u32[]{:S(2)}) %all-to-all-start) | async-done | bytes 393248 | tf_op jit(solution)/shard_map/all_to_all | solution.py:33
  37.6 0.2 convolution_convert_fusion
  37.9 0.9 copy.67
  38.8 8.3 %all-to-all-start.1 = ((bf16[32,48,128]{2,1,0:T(8,128)(2,1)}), bf16[32,48,128]{2,1,0:T(8,128)(2,1)S(1)}, u32[]{:S(2)}, u32[]{:S(2)}) async-start(bf16[32,48,128]{2,1,0:T(8,128)(2,1)} %copy.67), calls=%async_computation.1 | async-start | bytes 786432 | tf_op jit(solution)/shard_map/all_to_all | solution.py:36
  47.2 0.7 copy.69
  47.8 0.4 fusion.54
  48.2 0.1 divide_convert_fusion.2
  48.3 0.4 fusion.57
  48.7 10.3 %all-to-all-done.1 = bf16[32,48,128]{2,1,0:T(8,128)(2,1)S(1)} async-done(((bf16[32,48,128]{2,1,0:T(8,128)(2,1)}), bf16[32,48,128]{2,1,0:T(8,128)(2,1)S(1)}, u32[]{:S(2)}, u32[]{:S(2)}) %all-to-all-start.1) | async-done | bytes 393248 | tf_op jit(solution)/shard_map/all_to_all | solution.py:36
  59.1 0.1 reshape.63
  59.1 0.2 multiply_reduce_fusion
  59.4 0.3 fusion.25
  59.8 0.4 fusion.13
  60.1 34.2 %all-gather.2.cloned.1.call-done.pair_ref = bf16[8192,256]{1,0:T(8,128)(2,1)} async-done(((bf16[256,256]{1,0:T(8,128)(2,1)}), bf16[8192,256]{1,0:T(8,128)(2,1)}) %all-gather.2.cloned.1.call-update) | async-done | bytes 4194320 | tf_op jit(solution)/shard_map/all_gather | solution.py:118
  94.4 7.2 %shard_map.85 = f32[512,128]{1,0:T(8,128)} custom-call(s32[1]{0:T(128)} %bitcast.12.place_ref, bf16[512,128]{1,0:T(8,128)(2,1)} %bitcast.72, bf16[8192,256]{1,0:T(8,128)(2,1)} %all-gather.2.cloned.1.call-done.pair_ref), custom_call_target="tpu_custom_call" | custom-call | tf_op jit(solution)/shard_map/pallas_call | solution.py:94
  101.6 1.7 %fusion.22 = f32[]{:T(128)} fusion(f32[128,4,128]{2,0,1:T(8,128)} %bitcast.68, f32[4,256,128]{2,1,0:T(8,128)S(1)} %get-tuple-element.31, s32[]{:T(128)S(6)} %select_n.13, f32[4,128]{1,0:T(4,128)S(1)} %constant_dynamic-slice_fusion), kind=kLoop, calls=%fused_computation.40 | loop fusion | flops 393215 | bytes 526344 | tf_op jit(solution)/shard_map/reduce_sum | solution.py:144
  103.3 1.3 broadcast_in_dim.15
  104.6 21.5 %all-to-all-start.2 = ((f32[256,1,128]{2,1,0:T(1,128)}), f32[256,1,128]{2,1,0:T(1,128)S(1)}, u32[]{:S(2)}, u32[]{:S(2)}) async-start(f32[256,1,128]{2,1,0:T(1,128)} %broadcast_in_dim.15), calls=%async_computation.2 | async-start | bytes 262144 | tf_op jit(solution)/shard_map/all_to_all | solution.py:145
  126.1 0.9 copy.71
  127.0 1.8 %copy.72 = f32[1,128,4,128]{3,2,1,0:T(4,128)} copy(f32[1,128,4,128]{3,1,2,0:T(8,128)} %bitcast.69) | data formatting | bytes 524288
  128.8 10.1 %all-to-all-done.2 = f32[256,1,128]{2,1,0:T(1,128)S(1)} async-done(((f32[256,1,128]{2,1,0:T(1,128)}), f32[256,1,128]{2,1,0:T(1,128)S(1)}, u32[]{:S(2)}, u32[]{:S(2)}) %all-to-all-start.2) | async-done | bytes 131104 | tf_op jit(solution)/shard_map/all_to_all | solution.py:145
  138.9 0.9 slice_reduce_fusion
  (6 shorter events, 0.1 us)
Async XLA Ops:
  7.2 1.8 %copy-start = (bf16[4,128,128]{2,1,0:T(8,128)(2,1)S(1)}, bf16[4,128,128]{2,1,0:T(8,128)(2,1)}, u32[]{:S(2)}) copy-start(bf16[4,128,128]{2,1,0:T(8,128)(2,1)} %param.10) | copy-start | bytes 393220
  7.2 4.6 %copy-start.1 = (bf16[256,1,128]{2,0,1:T(8,128)(2,1)S(1)}, bf16[256,1,128]{2,0,1:T(8,128)(2,1)}, u32[]{:S(2)}) copy-start(bf16[256,1,128]{2,0,1:T(8,128)(2,1)} %param.8) | copy-start | bytes 196612
  7.2 18.0 %copy-start.4 = (s32[32]{0:T(128)S(1)}, s32[32]{0:T(128)}, u32[]{:S(2)}) copy-start(s32[32]{0:T(128)} %param.11) | copy-start | bytes 388
  7.2 19.3 %copy-start.2 = (bf16[256,4,128]{2,1,0:T(4,128)(2,1)S(1)}, bf16[256,4,128]{2,1,0:T(4,128)(2,1)}, u32[]{:S(2)}) copy-start(bf16[256,4,128]{2,1,0:T(4,128)(2,1)} %param.6) | copy-start | bytes 786436
  7.2 19.3 %copy-start.3 = (bf16[4,128,128]{2,1,0:T(8,128)(2,1)S(1)}, bf16[4,128,128]{2,1,0:T(8,128)(2,1)}, u32[]{:S(2)}) copy-start(bf16[4,128,128]{2,1,0:T(8,128)(2,1)} %param.9) | copy-start | bytes 393220
  7.2 87.1 %all-gather.2.cloned.1.call-start = ((), (), s32[]{:S(2)}) async-start(), calls=%async_computation.3 | async-start | bytes 4325376 | tf_op jit(solution)/shard_map/all_gather | solution.py:118
  13.2 24.5 %all-to-all-start = ((bf16[32,48,128]{2,1,0:T(8,128)(2,1)}), bf16[32,48,128]{2,1,0:T(8,128)(2,1)S(1)}, u32[]{:S(2)}, u32[]{:S(2)}) async-start(bf16[32,48,128]{2,1,0:T(8,128)(2,1)} %copy.65), calls=%async_computation | async-start | bytes 786432 | tf_op jit(solution)/shard_map/all_to_all | solution.py:33
  38.8 20.2 %all-to-all-start.1 = ((bf16[32,48,128]{2,1,0:T(8,128)(2,1)}), bf16[32,48,128]{2,1,0:T(8,128)(2,1)S(1)}, u32[]{:S(2)}, u32[]{:S(2)}) async-start(bf16[32,48,128]{2,1,0:T(8,128)(2,1)} %copy.67), calls=%async_computation.1 | async-start | bytes 786432 | tf_op jit(solution)/shard_map/all_to_all | solution.py:36
  104.6 34.3 %all-to-all-start.2 = ((f32[256,1,128]{2,1,0:T(1,128)}), f32[256,1,128]{2,1,0:T(1,128)S(1)}, u32[]{:S(2)}, u32[]{:S(2)}) async-start(f32[256,1,128]{2,1,0:T(1,128)} %broadcast_in_dim.15), calls=%async_computation.2 | async-start | bytes 262144 | tf_op jit(solution)/shard_map/all_to_all | solution.py:145
Sparse Core Ops, SparseCore 0:
  11.2 83.1 all-gather.1
